TPU v7x, 32 devices: a whole 2x2x4 slice. The times are simulated.
32 devices in a mesh: dp: 4 (over y, core), fsdp: 8 (over z, x).
Axes of the slice: x: 2, y: 2, z: 4, core: 2. Of those that a mesh axis runs over, the one named last changes fastest.
Arguments:
- hidden_in: bfloat16 [20480, 768], P(('dp', 'fsdp')), may hold values from -7 to 7
- prev_logits: bfloat16 [32, 12, 640, 640], P(('dp', 'fsdp')), may hold values from -6 to 6
- segment_ids: int32 [32, 640], P(('dp', 'fsdp')), may hold values from 0 to 3, never falling along the last dimension, each value on 1 to 320 neighbouring positions
- d_hidden: bfloat16 [20480, 768], P(('dp', 'fsdp')), may hold values from -6 to 6
- d_logits: bfloat16 [32, 12, 640, 640], P(('dp', 'fsdp')), may hold values from -3 to 3
- weight_in: float32 [768, 5376], P(('dp', 'fsdp')), may hold values from -2.5 to 2.5
- weight_out: float32 [3840, 768], P(('dp', 'fsdp')), may hold values from -2 to 2
- vectors: float32 [12, 768], P(None, ('dp', 'fsdp')), may hold values from -0.6 to 1.45
- moment_in: float32 [768, 5376], P(('dp', 'fsdp')), may hold values from -0.55 to 0.55
- moment_out: float32 [3840, 768], P(('dp', 'fsdp')), may hold values from -0.55 to 0.55
- moment_vectors: float32 [12, 768], P(None, ('dp', 'fsdp')), may hold values from -1.5 to 1.5
- square_in: float32 [768, 5376], P(('dp', 'fsdp')), may hold values from 0.001 to 0.004
- square_out: float32 [3840, 768], P(('dp', 'fsdp')), may hold values from 0.001 to 0.004
- square_vectors: float32 [12, 768], P(None, ('dp', 'fsdp')), may hold values from 0.008 to 0.032
- step_count: int32 [1], replicated, may hold values from 1 to 20
Outputs:
- hidden_out: bfloat16 [20480, 768], P(('dp', 'fsdp'))
- logits: bfloat16 [32, 12, 640, 640], P(('dp', 'fsdp'))
- d_input: bfloat16 [20480, 768], P(('dp', 'fsdp'))
- d_prev: bfloat16 [32, 12, 640, 640], P(('dp', 'fsdp'))
- grad_weight_in: float32 [768, 5376], P(('dp', 'fsdp'))
- grad_weight_out: float32 [3840, 768], P(('dp', 'fsdp'))
- grad_vectors: float32 [12, 768], P(None, ('dp', 'fsdp'))
- new_moment_in: float32 [768, 5376], P(('dp', 'fsdp'))
- new_moment_out: float32 [3840, 768], P(('dp', 'fsdp'))
- new_moment_vectors: float32 [12, 768], P(None, ('dp', 'fsdp'))
- new_square_in: float32 [768, 5376], P(('dp', 'fsdp'))
- new_square_out: float32 [3840, 768], P(('dp', 'fsdp'))
- new_square_vectors: float32 [12, 768], P(None, ('dp', 'fsdp'))
- new_weight_in: float32 [768, 5376], P(('dp', 'fsdp'))
- new_weight_out: float32 [3840, 768], P(('dp', 'fsdp'))
- new_vectors: float32 [12, 768], P(None, ('dp', 'fsdp'))
- copy_weight_in: bfloat16 [768, 5376], P(('dp', 'fsdp'))
- copy_weight_out: bfloat16 [3840, 768], P(('dp', 'fsdp'))
- copy_vectors: bfloat16 [12, 768], P(None, ('dp', 'fsdp'))
- grad_norm: float32 [], replicated
Inputs may be any that keep to these rules, and one draw needn't show every extreme that they name: `segment_ids`: along each row the segment numbers never fall; no segment holds more than 320 slots.
All inputs are finite; a program needn't handle non-finite values.
Results may differ from a plain program's by a relative error of at most 0.012.
Values may be sent and summed in bfloat16 or wider, within the bound.
A program may use at most 192 MiB of HBM per device.

v0:
```python
import math
import jax
import jax.numpy as jnp
from jax import lax
from jax.sharding import PartitionSpec as P

PARAMS = 7087104
norm_eps = 1e-12
clip_scale = 1.0
beta_one = 0.9
beta_two = 0.999
adam_eps = 1e-08
rate_matrix = 0.06
rate_vector = 0.25
decay_matrix = 0.01
masked_fill = -1e30


def gelu_exact(upward):
    return jax.nn.gelu(upward, approximate=False)


def norm_rows(residual, gain_row, shift_row):
    centered = residual - jnp.mean(residual, axis=1, keepdims=True)
    scaling = lax.rsqrt(jnp.mean(centered * centered, axis=1, keepdims=True) + norm_eps)
    normed = centered * scaling
    return (normed * gain_row + shift_row, normed, scaling)


def norm_back(grad_after, normed, scaling, gain_row):
    scaled_grad = grad_after * gain_row
    return scaling * (
        scaled_grad
        - jnp.mean(scaled_grad, axis=1, keepdims=True)
        - normed * jnp.mean(scaled_grad * normed, axis=1, keepdims=True)
    )


def split_heads(matrix, head_count):
    return matrix.reshape(matrix.shape[0], head_count, -1)


def forward(weights, tokens, previous, same_doc):
    weight_in, weight_out, vectors = weights
    model_width = weight_out.shape[1]
    head_count = previous.shape[0]
    row_count = tokens.shape[0]
    score_scale = (model_width // head_count) ** (-0.5)
    vector_rows = vectors.astype(jnp.float32)
    projected = jnp.dot(tokens, weight_in[:, : 3 * model_width], preferred_element_type=jnp.float32)
    queries = (projected[:, :model_width] + vector_rows[4]).astype(jnp.bfloat16)
    keys_low = projected[:, model_width : 2 * model_width].astype(jnp.bfloat16)
    values_low = (projected[:, 2 * model_width :] + vector_rows[5]).astype(jnp.bfloat16)
    scores = jnp.einsum(
        "qhd,khd->hqk",
        split_heads(queries, head_count),
        split_heads(keys_low, head_count),
        preferred_element_type=jnp.float32,
    ) * score_scale + previous.astype(jnp.float32)
    masked = jnp.where(same_doc[None], scores, masked_fill)
    row_max = jnp.max(masked, axis=2, keepdims=True)
    expo_terms = jnp.exp(masked - row_max)
    totals = jnp.sum(expo_terms, axis=2, keepdims=True)
    attn_probs = expo_terms / totals
    log_sums = row_max + jnp.log(totals)
    mixed_heads = jnp.einsum(
        "hqk,khd->qhd",
        attn_probs.astype(jnp.bfloat16),
        split_heads(values_low, head_count),
        preferred_element_type=jnp.float32,
    )
    mixed_heads = mixed_heads.reshape(row_count, model_width).astype(jnp.bfloat16)
    first_sum = tokens.astype(jnp.float32) + (
        jnp.dot(mixed_heads, weight_out[:model_width], preferred_element_type=jnp.float32)
        + vector_rows[6]
    )
    hidden_one, normed_one, scale_one = norm_rows(first_sum, vector_rows[0], vector_rows[2])
    hidden_low = hidden_one.astype(jnp.bfloat16)
    upward = jnp.dot(
        hidden_low, weight_in[:, 3 * model_width :], preferred_element_type=jnp.float32
    ) + vector_rows[8:].reshape(-1)
    activated = gelu_exact(upward).astype(jnp.bfloat16)
    second_sum = hidden_one + (
        jnp.dot(activated, weight_out[model_width:], preferred_element_type=jnp.float32)
        + vector_rows[7]
    )
    output, normed_two, scale_two = norm_rows(second_sum, vector_rows[1], vector_rows[3])
    kept_values = (
        queries,
        keys_low,
        values_low,
        log_sums,
        mixed_heads,
        normed_one,
        scale_one,
        hidden_low,
        upward,
        activated,
        normed_two,
        scale_two,
    )
    return (output, scores, kept_values)


def backward(weights, kept_values, tokens, previous, same_doc, grad_hidden, grad_logits):
    weight_in, weight_out, vectors = weights
    (
        queries,
        keys_low,
        values_low,
        log_sums,
        mixed_heads,
        normed_one,
        scale_one,
        hidden_low,
        upward,
        activated,
        normed_two,
        scale_two,
    ) = kept_values
    model_width = weight_out.shape[1]
    head_count = previous.shape[0]
    row_count = tokens.shape[0]
    score_scale = (model_width // head_count) ** (-0.5)
    vector_rows = vectors.astype(jnp.float32)
    grad_output = grad_hidden.astype(jnp.float32)
    gain_two_grad = jnp.sum(grad_output * normed_two, axis=0)
    shift_two_grad = jnp.sum(grad_output, axis=0)
    grad_second = norm_back(grad_output, normed_two, scale_two, vector_rows[1])
    grad_down = grad_second.astype(jnp.bfloat16)
    bias_down_grad = jnp.sum(grad_down, axis=0, dtype=jnp.float32)
    down_grad = jnp.einsum("tf,td->fd", activated, grad_down, preferred_element_type=jnp.float32)
    grad_activated = jnp.einsum(
        "td,fd->tf", grad_down, weight_out[model_width:], preferred_element_type=jnp.float32
    )
    unused_value, gelu_pull = jax.vjp(gelu_exact, upward)
    grad_up = gelu_pull(grad_activated)[0].astype(jnp.bfloat16)
    bias_up_grad = jnp.sum(grad_up, axis=0, dtype=jnp.float32)
    up_grad = jnp.einsum("td,tf->df", hidden_low, grad_up, preferred_element_type=jnp.float32)
    grad_hidden_one = grad_second + jnp.einsum(
        "tf,df->td", grad_up, weight_in[:, 3 * model_width :], preferred_element_type=jnp.float32
    )
    gain_one_grad = jnp.sum(grad_hidden_one * normed_one, axis=0)
    shift_one_grad = jnp.sum(grad_hidden_one, axis=0)
    grad_first = norm_back(grad_hidden_one, normed_one, scale_one, vector_rows[0])
    grad_attn = grad_first.astype(jnp.bfloat16)
    bias_out_grad = jnp.sum(grad_attn, axis=0, dtype=jnp.float32)
    attn_grad = jnp.einsum("tc,td->cd", mixed_heads, grad_attn, preferred_element_type=jnp.float32)
    grad_mixed = jnp.einsum(
        "td,cd->tc", grad_attn, weight_out[:model_width], preferred_element_type=jnp.float32
    ).astype(jnp.bfloat16)
    head_queries = split_heads(queries, head_count)
    head_keys = split_heads(keys_low, head_count)
    head_values = split_heads(values_low, head_count)
    head_grad_mixed = split_heads(grad_mixed, head_count)
    scores = jnp.einsum(
        "qhd,khd->hqk", head_queries, head_keys, preferred_element_type=jnp.float32
    ) * score_scale + previous.astype(jnp.float32)
    attn_probs = jnp.exp(jnp.where(same_doc[None], scores, masked_fill) - log_sums)
    grad_probs = jnp.einsum(
        "qhd,khd->hqk", head_grad_mixed, head_values, preferred_element_type=jnp.float32
    )
    grad_scores = attn_probs * (
        grad_probs - jnp.sum(attn_probs * grad_probs, axis=2, keepdims=True)
    )
    grad_total = (grad_scores + grad_logits.astype(jnp.float32)).astype(jnp.bfloat16)
    grad_queries = (
        (
            jnp.einsum("hqk,khd->qhd", grad_total, head_keys, preferred_element_type=jnp.float32)
            * score_scale
        )
        .astype(jnp.bfloat16)
        .reshape(row_count, model_width)
    )
    grad_keys = (
        (
            jnp.einsum("hqk,qhd->khd", grad_total, head_queries, preferred_element_type=jnp.float32)
            * score_scale
        )
        .astype(jnp.bfloat16)
        .reshape(row_count, model_width)
    )
    grad_values = (
        jnp.einsum(
            "hqk,qhd->khd",
            attn_probs.astype(jnp.bfloat16),
            head_grad_mixed,
            preferred_element_type=jnp.float32,
        )
        .astype(jnp.bfloat16)
        .reshape(row_count, model_width)
    )
    grad_projected = jnp.concatenate([grad_queries, grad_keys, grad_values], axis=1)
    qkv_grad = jnp.einsum("td,tc->dc", tokens, grad_projected, preferred_element_type=jnp.float32)
    grad_tokens = grad_first + jnp.einsum(
        "tc,dc->td",
        grad_projected,
        weight_in[:, : 3 * model_width],
        preferred_element_type=jnp.float32,
    )
    small_rows = jnp.stack(
        [
            gain_one_grad,
            gain_two_grad,
            shift_one_grad,
            shift_two_grad,
            jnp.sum(grad_queries, axis=0, dtype=jnp.float32),
            jnp.sum(grad_values, axis=0, dtype=jnp.float32),
            bias_out_grad,
            bias_down_grad,
        ]
    )
    small_grads = jnp.concatenate([small_rows, bias_up_grad.reshape(-1, model_width)], axis=0)
    return (
        jnp.concatenate([qkv_grad, up_grad], axis=1),
        jnp.concatenate([attn_grad, down_grad], axis=0),
        small_grads,
        grad_tokens.astype(jnp.bfloat16),
        grad_total,
    )


def adam_update(master, moment, square, gradient, factor, step_value, step_rate, decay_rate):
    clipped = gradient * factor
    new_moment = beta_one * moment + (1.0 - beta_one) * clipped
    new_square = beta_two * square + (1.0 - beta_two) * clipped * clipped
    fixed_moment = new_moment / (1.0 - jnp.power(beta_one, step_value))
    fixed_square = new_square / (1.0 - jnp.power(beta_two, step_value))
    updated = master - step_rate * (
        fixed_moment / (jnp.sqrt(fixed_square) + adam_eps) + decay_rate * master
    )
    return (clipped, new_moment, new_square, updated)


def body(
    hidden_in,
    prev_logits,
    segment_ids,
    d_hidden,
    d_logits,
    weight_in,
    weight_out,
    vectors,
    moment_in,
    moment_out,
    moment_vectors,
    square_in,
    square_out,
    square_vectors,
    step_count,
):
    low_in = weight_in.astype(jnp.bfloat16)
    low_out = weight_out.astype(jnp.bfloat16)
    low_small = vectors.astype(jnp.bfloat16)
    gathered = (
        lax.all_gather(low_in, ("dp", "fsdp"), axis=0, tiled=True),
        lax.all_gather(low_out, ("dp", "fsdp"), axis=0, tiled=True),
        lax.all_gather(low_small, ("dp", "fsdp"), axis=1, tiled=True),
    )
    segments = segment_ids[0]
    same_doc = segments[:, None] == segments[None, :]
    previous = prev_logits[0]
    output, scores, kept_values = forward(gathered, hidden_in, previous, same_doc)
    regathered = (
        lax.all_gather(low_in, ("dp", "fsdp"), axis=0, tiled=True),
        lax.all_gather(low_out, ("dp", "fsdp"), axis=0, tiled=True),
        lax.all_gather(low_small, ("dp", "fsdp"), axis=1, tiled=True),
    )
    unused_out, unused_scores, again_values = forward(regathered, hidden_in, previous, same_doc)
    full_in, full_out, full_small, grad_tokens, grad_prev = backward(
        regathered, again_values, hidden_in, previous, same_doc, d_hidden, d_logits[0]
    )
    owned_in, owned_out, owned_small = (
        lax.psum_scatter(full_in, ("dp", "fsdp"), scatter_dimension=0, tiled=True),
        lax.psum_scatter(full_out, ("dp", "fsdp"), scatter_dimension=0, tiled=True),
        lax.psum_scatter(full_small, ("dp", "fsdp"), scatter_dimension=1, tiled=True),
    )
    local_squares = (
        jnp.sum(owned_in * owned_in)
        + jnp.sum(owned_out * owned_out)
        + jnp.sum(owned_small * owned_small)
    )
    total_squares = lax.psum(local_squares, ("dp", "fsdp"))
    grad_norm = jnp.sqrt(total_squares)
    threshold = clip_scale * math.sqrt(PARAMS)
    factor = jnp.minimum(1.0, threshold / (grad_norm + 1e-06))
    step_value = step_count[0].astype(jnp.float32)
    clip_in, moment_one, square_one, updated_in = adam_update(
        weight_in, moment_in, square_in, owned_in, factor, step_value, rate_matrix, decay_matrix
    )
    clip_out, moment_two, square_two, updated_out = adam_update(
        weight_out, moment_out, square_out, owned_out, factor, step_value, rate_matrix, decay_matrix
    )
    clip_small, moment_three, square_three, updated_small = adam_update(
        vectors, moment_vectors, square_vectors, owned_small, factor, step_value, rate_vector, 0.0
    )
    return (
        output.astype(jnp.bfloat16),
        scores.astype(jnp.bfloat16)[None],
        grad_tokens,
        grad_prev[None],
        clip_in,
        clip_out,
        clip_small,
        moment_one,
        moment_two,
        moment_three,
        square_one,
        square_two,
        square_three,
        updated_in,
        updated_out,
        updated_small,
        updated_in.astype(jnp.bfloat16),
        updated_out.astype(jnp.bfloat16),
        updated_small.astype(jnp.bfloat16),
        grad_norm,
    )


def solution(mesh):
    return jax.shard_map(
        body,
        mesh=mesh,
        in_specs=(
            P(("dp", "fsdp"), None),
            P(("dp", "fsdp"), None, None, None),
            P(("dp", "fsdp"), None),
            P(("dp", "fsdp"), None),
            P(("dp", "fsdp"), None, None, None),
            P(("dp", "fsdp"), None),
            P(("dp", "fsdp"), None),
            P(None, ("dp", "fsdp")),
            P(("dp", "fsdp"), None),
            P(("dp", "fsdp"), None),
            P(None, ("dp", "fsdp")),
            P(("dp", "fsdp"), None),
            P(("dp", "fsdp"), None),
            P(None, ("dp", "fsdp")),
            P(),
        ),
        out_specs=(
            P(("dp", "fsdp"), None),
            P(("dp", "fsdp"), None, None, None),
            P(("dp", "fsdp"), None),
            P(("dp", "fsdp"), None, None, None),
            P(("dp", "fsdp"), None),
            P(("dp", "fsdp"), None),
            P(None, ("dp", "fsdp")),
            P(("dp", "fsdp"), None),
            P(("dp", "fsdp"), None),
            P(None, ("dp", "fsdp")),
            P(("dp", "fsdp"), None),
            P(("dp", "fsdp"), None),
            P(None, ("dp", "fsdp")),
            P(("dp", "fsdp"), None),
            P(("dp", "fsdp"), None),
            P(None, ("dp", "fsdp")),
            P(("dp", "fsdp"), None),
            P(("dp", "fsdp"), None),
            P(None, ("dp", "fsdp")),
            P(),
        ),
        check_vma=False,
    )
```

profile of v0, /device:TPU:0, one launch (start us, length us, event | category | flops | bytes accessed | tf_op | source)
XLA Modules:
  0.0 645.5 jit_solution(6729992086085996024)
XLA Ops:
  7.2 1.8 convert_element_type.143
  9.1 1.7 convert_element_type.154
  10.8 0.7 convert_bitcast_fusion.1
  11.5 71.6 %all-gather = bf16[32,24,12]{1,2,0:T(8,128)(2,1)S(1)} all-gather(bf16[1,24,12]{1,2,0:T(8,128)(2,1)S(1)} %convert_bitcast_fusion.1), channel_id=1, replica_groups=mesh['dp'=4,'fsdp'=8] {'dp','fsdp'}, dimensions={0}, use_global_device_ids=true | all-gather | bytes 19008 | tf_op jit(solution)/shard_map/all_gather | solution.py:258
  83.5 14.0 %copy.85 = bf16[1,12,640,640]{2,3,1,0:T(8,128)(2,1)} copy(bf16[1,12,640,640]{3,2,1,0:T(8,128)(2,1)} %param.16) | data formatting | bytes 19660800 | tf_op args[1]
  98.0 4.5 fusion.34
  102.6 1.3 fusion.45
  105.2 1.9 copy.82
  107.1 11.9 %select_reduce_fusion = (f32[12,640]{1,0:T(8,128)S(1)}, f32[12,640,640]{1,2,0:T(8,128)}) fusion(pred[640,640]{0,1:T(8,128)(4,1)S(1)} %broadcast_compare_fusion, bf16[1,12,640,640]{2,3,1,0:T(8,128)(2,1)} %copy.85, bf16[640,12,64]{0,2,1:T(8,128)(2,1)S(1)} %bitcast.63, bf16[640,12,64]{0,2,1:T(8,128)(2,1)S(1)} %bitcast.61), kind=kOutput, calls=%fused_computation.11 | convolution fusion | flops 653713920 | bytes 31897600 | tf_op jit(solution)/shard_map/qhd,khd->hqk/dot_general | solution.py:54
  119.0 17.7 %convert_bitcast_fusion = (bf16[1,12,640,640]{2,3,1,0:T(8,128)(2,1)}, f32[12,640]{1,0:T(8,128)S(1)}) fusion(f32[12,640,640]{1,2,0:T(8,128)} %get-tuple-element.143, f32[12,640]{1,0:T(8,128)S(1)} %get-tuple-element.142, pred[640,640]{0,1:T(8,128)(4,1)S(1)} %broadcast_compare_fusion), kind=kLoop, calls=%fused_computation.18 | loop fusion | flops 19653120 | bytes 29962240 | tf_op jit(solution)/shard_map/broadcast_in_dim | solution.py:299
  136.8 10.8 %fusion.55 = bf16[12,64,640]{2,1,0:T(8,128)(2,1)} fusion(bf16[640,12,64]{0,2,1:T(8,128)(2,1)S(1)} %bitcast.67, f32[12,640,640]{1,2,0:T(8,128)} %get-tuple-element.143, f32[12,640]{1,0:T(8,128)S(1)} %get-tuple-element.138, f32[12,640]{1,0:T(8,128)S(1)} %get-tuple-element.142, pred[640,640]{0,1:T(8,128)(4,1)S(1)} %broadcast_compare_fusion), kind=kOutput, calls=%fused_computation.92 | convolution fusion | flops 649297920 | bytes 22097920 | tf_op jit(solution)/shard_map/hqk,khd->qhd/dot_general | solution.py:66
  147.6 14.3 %all-gather.6.cloned.1.call-done = bf16[3840,768]{1,0:T(8,128)(2,1)} async-done(((bf16[120,768]{1,0:T(8,128)(2,1)}), bf16[3840,768]{1,0:T(8,128)(2,1)}) %all-gather.6.cloned.1.call-update) | async-done | bytes 5898256 | tf_op jit(solution)/shard_map/all_gather | solution.py:257
  161.9 3.1 fusion.86
  165.4 23.9 %multiply_convert_fusion = (bf16[640,3072]{1,0:T(8,128)(2,1)S(1)}, f32[640,3072]{1,0:T(8,128)}, f32[640,3072]{1,0:T(8,128)}) fusion(f32[3072]{0:T(1024)S(1)} %add.219, bf16[768,5376]{1,0:T(8,128)(2,1)} %all-gather.4.cloned.1.call-done, f32[640,768]{1,0:T(8,128)S(1)} %get-tuple-element.145, f32[768]{0:T(1024)S(1)} %get-tuple-element.111, ...), kind=kOutput, calls=%fused_computation.27 | convolution fusion | flops 3152117760 | bytes 26369024 | tf_op jit(solution)/shard_map/dot_general | solution.py:79
  189.3 3.4 fusion.87
  193.2 1.0 fusion.44
  194.2 1.8 convert_reduce_fusion.2
  195.9 6.4 fusion.69
  202.3 10.9 %convert_reduce_fusion = (f32[3072]{0:T(1024)S(1)}, bf16[640,3072]{1,0:T(8,128)(2,1)S(1)}) fusion(f32[640,3072]{1,0:T(8,128)} %get-tuple-element.136, bf16[3840,768]{1,0:T(8,128)(2,1)} %all-gather.6.cloned.1.call-done, f32[640,768]{1,0:T(8,128)S(1)} %get-tuple-element.132, f32[640,3072]{1,0:T(8,128)} %get-tuple-element.146, f32[3072]{0:T(1024)S(1)} %add.219), kind=kOutput, calls=%fused_computation.25 | convolution fusion | flops 3053810688 | bytes 26370048 | tf_op jit(solution)/shard_map/td,fd->tf/dot_general | solution.py:133
  213.3 3.8 multiply_reduce_fusion.1
  217.7 1.3 copy-done.6
  219.0 2.5 fusion.66
  221.5 9.5 %pad_maximum_fusion.1 = f32[3840,768]{1,0:T(8,128)} fusion(f32[3072,768]{1,0:T(8,128)} %fusion.69, f32[768,768]{1,0:T(8,128)} %fusion.66), kind=kLoop, calls=%fused_computation.13 | loop fusion | flops 2949120 | bytes 23592960 | tf_op jit(solution)/shard_map/concatenate | solution.py:216
  231.1 15.4 %copy.88 = bf16[1,12,640,640]{2,3,1,0:T(8,128)(2,1)} copy(bf16[1,12,640,640]{3,2,1,0:T(8,128)(2,1)} %param.19) | data formatting | bytes 19660800 | tf_op args[4]
  246.5 3.0 convolution_convert_fusion
  249.6 1.3 copy.87
  250.9 28.2 %fusion.1 = bf16[12,640,640]{1,2,0:T(8,128)(2,1)} fusion(f32[12,640,640]{1,2,0:T(8,128)} %get-tuple-element.143, bf16[1,12,640,640]{2,3,1,0:T(8,128)(2,1)} %copy.88, f32[12,640]{1,0:T(8,128)S(1)} %log_add_fusion, pred[640,640]{0,1:T(8,128)(4,1)S(1)} %broadcast_compare_fusion, bf16[640,12,64]{0,2,1:T(8,128)(2,1)} %bitcast.73, bf16[640,12,64]{0,2,1:T(8,128)(2,1)} %bitcast.68), kind=kOutput, calls=%fused_computation.2 | convolution fusion | flops 1307451520 | bytes 41728000 | tf_op jit(solution)/shard_map/sub | solution.py:164
  279.2 5.8 convert_reduce_fusion.5
  284.9 1.8 copy-done
  287.0 3.2 multiply_convert_fusion.1
  290.2 11.5 %convert_reduce_fusion.4 = (f32[12,64]{1,0:T(8,128)S(1)}, bf16[12,64,640]{2,1,0:T(8,128)(2,1)S(1)}) fusion(bf16[640,12,64]{0,2,1:T(8,128)(2,1)S(1)} %bitcast.74, f32[12,640,640]{1,2,0:T(8,128)} %get-tuple-element.143, f32[12,640]{1,0:T(8,128)S(1)} %log_add_fusion, pred[640,640]{0,1:T(8,128)(4,1)S(1)} %broadcast_compare_fusion), kind=kOutput, calls=%fused_computation.73 | convolution fusion | flops 645364992 | bytes 22070272 | tf_op jit(solution)/shard_map/hqk,qhd->khd/dot_general | solution.py:184
  301.8 0.9 copy-done.30
  302.8 7.9 %convolution_bitcast_fusion = f32[768,2304]{0,1:T(8,128)} fusion(bf16[640,768]{1,0:T(8,128)(2,1)S(1)} %copy-done.29, bf16[640,768]{0,1:T(8,128)(2,1)S(1)} %bitcast.81, bf16[640,768]{0,1:T(8,128)(2,1)S(1)} %bitcast.69, bf16[640,768]{0,1:T(8,128)(2,1)S(1)} %bitcast.65), kind=kOutput, calls=%fused_computation.41 | convolution fusion | flops 2273771520 | bytes 11010048 | tf_op jit(solution)/shard_map/td,tc->dc/dot_general | solution.py:194
  310.7 8.2 %copy.92 = f32[768,2304]{1,0:T(8,128)} copy(f32[768,2304]{0,1:T(8,128)} %convolution_bitcast_fusion) | data formatting | bytes 14155776 | tf_op jit(solution)/shard_map/td,tc->dc/dot_general | solution.py:194
  318.9 6.6 %fusion.75 = f32[768,3072]{1,0:T(8,128)S(1)} fusion(bf16[640,3072]{1,0:T(8,128)(2,1)} %copy-done.9, f32[640,768]{1,0:T(8,128)S(1)} %get-tuple-element.145, f32[768]{0:T(1024)S(1)} %get-tuple-element.111, f32[768]{0:T(1024)S(1)} %get-tuple-element.112, f32[640]{0:T(1024)S(1)} %add_rsqrt_fusion.1, f32[640]{0:T(1024)S(1)} %broadcast_multiply_fusion.7), kind=kOutput, calls=%fused_computation.145 | convolution fusion | flops 3022356480 | bytes 15346688 | tf_op jit(solution)/shard_map/td,tf->df/dot_general | solution.py:139
  325.5 6.0 pad_maximum_fusion
  332.5 13.9 %copy.94 = bf16[1,12,640,640]{3,2,1,0:T(8,128)(2,1)} copy(bf16[1,12,640,640]{2,3,1,0:T(8,128)(2,1)} %bitcast.60) | data formatting | bytes 19660800
  346.4 39.7 %all-reduce = f32[12,768]{1,0:T(8,128)S(1)} all-reduce(f32[12,768]{1,0:T(8,128)S(1)} %concatenate.15), channel_id=4, replica_groups=mesh['dp'=4,'fsdp'=8] {'dp','fsdp'}, use_global_device_ids=true, to_apply=%region_24.25.clone | all-reduce | flops 9216 | bytes 73728
  386.2 0.7 multiply_reduce_fusion.8
  386.9 6.0 add_convert_fusion.1
  392.9 1.7 multiply_reduce_fusion.7
  394.6 180.7 %reduce-scatter.4.cloned.1.call-done = f32[24,5376]{1,0:T(8,128)} async-done(((f32[768,5376]{1,0:T(8,128)}), f32[24,5376]{1,0:T(8,128)}) %reduce-scatter.4.cloned.1.call-update) | async-done | bytes 516112 | tf_op jit(solution)/shard_map/reduce_scatter | solution.py:274
  575.4 1.8 multiply_reduce_fusion.6
  579.2 13.9 %copy.93 = bf16[1,12,640,640]{3,2,1,0:T(8,128)(2,1)} copy(bf16[1,12,640,640]{2,3,1,0:T(8,128)(2,1)} %get-tuple-element.137) | data formatting | bytes 19660800
  593.2 39.3 %psum.7 = f32[]{:T(128)} all-reduce(f32[]{:T(128)S(6)} %add.235), channel_id=1, replica_groups=mesh['dp'=4,'fsdp'=8] {'dp','fsdp'}, use_global_device_ids=true, to_apply=%region_26.27 | all-reduce | flops 1 | bytes 8 | tf_op jit(solution)/shard_map/psum | solution.py:283
  633.3 1.4 fusion.78
  634.7 1.2 fusion.80
  636.0 1.5 fusion.82
  (111 shorter events, 4.4 us)
Async XLA Ops:
  7.2 90.8 %all-gather.4.cloned.1.call-start = ((), (), s32[]{:S(2)}) async-start(), calls=%async_computation.2 | async-start | bytes 8515584 | tf_op jit(solution)/shard_map/all_gather | solution.py:256
  9.0 152.9 %all-gather.6.cloned.1.call-start = ((), (), s32[]{:S(2)}) async-start(), calls=%async_computation.3 | async-start | bytes 6082560 | tf_op jit(solution)/shard_map/all_gather | solution.py:257
  10.8 382.1 %reduce-scatter.6.cloned.1.call-start = ((), (), s32[]{:S(2)}) async-start(), calls=%async_computation.5 | async-start | bytes 12165120 | tf_op jit(solution)/shard_map/reduce_scatter | solution.py:275
  83.5 14.0 %copy-start.27 = (s32[1,640]{1,0:T(1,128)S(1)}, s32[1,640]{1,0:T(1,128)}, u32[]{:S(2)}) copy-start(s32[1,640]{1,0:T(1,128)} %param.17) | copy-start | bytes 7684
  83.5 14.4 %copy-start.28 = (bf16[640,768]{1,0:T(8,128)(2,1)S(1)}, bf16[640,768]{1,0:T(8,128)(2,1)}, u32[]{:S(2)}) copy-start(bf16[640,768]{1,0:T(8,128)(2,1)} %param.15) | copy-start | bytes 2949124
  104.5 14.5 %copy-start.4 = (bf16[640,768]{0,1:T(8,128)(2,1)}, bf16[640,768]{0,1:T(8,128)(2,1)S(1)}, u32[]{:S(2)}) copy-start(bf16[640,768]{0,1:T(8,128)(2,1)S(1)} %copy.83) | copy-start | bytes 2949124
  105.2 13.9 %copy-start.2 = (bf16[640,768]{0,1:T(8,128)(2,1)}, bf16[640,768]{0,1:T(8,128)(2,1)S(1)}, u32[]{:S(2)}) copy-start(bf16[640,768]{0,1:T(8,128)(2,1)S(1)} %copy.84) | copy-start | bytes 2949124
  107.1 29.7 %copy-start.16 = (bf16[640,768]{0,1:T(8,128)(2,1)}, bf16[640,768]{0,1:T(8,128)(2,1)S(1)}, u32[]{:S(2)}) copy-start(bf16[640,768]{0,1:T(8,128)(2,1)S(1)} %copy.82) | copy-start | bytes 2949124
  161.9 27.4 %slice-start.2 = ((s8[5898240]{0:T(1024)(128)(4,1)}), s8[4194304]{0:T(1024)(128)(4,1)S(1)}, s32[]{:S(2)}) async-start(s8[5898240]{0:T(1024)(128)(4,1)} %bitcast.79), calls=%async_computation.8 | async-start | bytes 8388608
  165.4 23.9 %slice-start.3 = ((s8[5898240]{0:T(1024)(128)(4,1)}), s8[1703936]{0:T(1024)(128)(4,1)S(1)}, s32[]{:S(2)}) async-start(s8[5898240]{0:T(1024)(128)(4,1)} %bitcast.79), calls=%async_computation.9 | async-start | bytes 3407872
  189.3 3.8 copy-start.8
  195.9 17.3 %slice-start = ((s8[8257536]{0:T(1024)(128)(4,1)}), s8[4194304]{0:T(1024)(128)(4,1)S(1)}, s32[]{:S(2)}) async-start(s8[8257536]{0:T(1024)(128)(4,1)} %bitcast.77), calls=%async_computation.6 | async-start | bytes 8388608
  202.3 10.9 %slice-start.1 = ((s8[8257536]{0:T(1024)(128)(4,1)}), s8[4063232]{0:T(1024)(128)(4,1)S(1)}, s32[]{:S(2)}) async-start(s8[8257536]{0:T(1024)(128)(4,1)} %bitcast.77), calls=%async_computation.7 | async-start | bytes 8126464
  213.2 3.8 copy-start.9
  213.2 5.8 copy-start.18
  217.7 1.3 copy-start.6
  231.0 344.4 %reduce-scatter.4.cloned.1.call-start = ((), (), s32[]{:S(2)}) async-start(), calls=%async_computation.4 | async-start | bytes 17031168 | tf_op jit(solution)/shard_map/reduce_scatter | solution.py:274
  250.9 28.3 %copy-start.3 = (bf16[640,768]{0,1:T(8,128)(2,1)S(1)}, bf16[640,768]{0,1:T(8,128)(2,1)}, u32[]{:S(2)}) copy-start(bf16[640,768]{0,1:T(8,128)(2,1)} %copy-done.2) | copy-start | bytes 2949124
  279.2 7.6 %copy-start = (bf16[12,640,640]{1,2,0:T(8,128)(2,1)S(1)}, bf16[12,640,640]{1,2,0:T(8,128)(2,1)}, u32[]{:S(2)}) copy-start(bf16[12,640,640]{1,2,0:T(8,128)(2,1)} %fusion.1) | copy-start | bytes 29491204
  279.2 7.8 %copy-start.5 = (bf16[640,768]{0,1:T(8,128)(2,1)S(1)}, bf16[640,768]{0,1:T(8,128)(2,1)}, u32[]{:S(2)}) copy-start(bf16[640,768]{0,1:T(8,128)(2,1)} %copy-done.4) | copy-start | bytes 2949124
  287.0 14.8 %copy-start.10 = (bf16[12,64,640]{2,1,0:T(8,128)(2,1)}, bf16[12,64,640]{2,1,0:T(8,128)(2,1)S(1)}, u32[]{:S(2)}) copy-start(bf16[12,64,640]{2,1,0:T(8,128)(2,1)S(1)} %get-tuple-element.151) | copy-start | bytes 2949124
  287.0 3.2 copy-start.19
  290.2 11.6 %copy-start.17 = (bf16[12,64,640]{2,1,0:T(8,128)(2,1)}, bf16[12,64,640]{2,1,0:T(8,128)(2,1)S(1)}, u32[]{:S(2)}) copy-start(bf16[12,64,640]{2,1,0:T(8,128)(2,1)S(1)} %multiply_convert_fusion.1) | copy-start | bytes 2949124
  290.2 12.5 %copy-start.29 = (bf16[640,768]{1,0:T(8,128)(2,1)S(1)}, bf16[640,768]{1,0:T(8,128)(2,1)}, u32[]{:S(2)}) copy-start(bf16[640,768]{1,0:T(8,128)(2,1)} %param.15) | copy-start | bytes 2949124
  301.8 1.0 copy-start.30
  318.8 6.6 %copy-start.1 = (f32[768,2304]{1,0:T(8,128)S(1)}, f32[768,2304]{1,0:T(8,128)}, u32[]{:S(2)}) copy-start(f32[768,2304]{1,0:T(8,128)} %copy.92) | copy-start | bytes 21233668
  332.4 54.4 %copy-start.7 = (f32[640,768]{1,0:T(8,128)S(1)}, f32[640,768]{1,0:T(8,128)}, u32[]{:S(2)}) copy-start(f32[640,768]{1,0:T(8,128)} %copy-done.6) | copy-start | bytes 5898244
  332.5 54.4 %copy-start.11 = (bf16[12,64,640]{2,1,0:T(8,128)(2,1)S(1)}, bf16[12,64,640]{2,1,0:T(8,128)(2,1)}, u32[]{:S(2)}) copy-start(bf16[12,64,640]{2,1,0:T(8,128)(2,1)} %copy-done.10) | copy-start | bytes 2949124
  386.2 6.7 %copy-start.24 = (f32[12,768]{1,0:T(8,128)}, f32[12,768]{1,0:T(8,128)S(1)}, u32[]{:S(2)}) copy-start(f32[12,768]{1,0:T(8,128)S(1)} %all-reduce) | copy-start | bytes 110596
  579.1 54.1 %copy-start.25 = (f32[12,24]{1,0:T(8,128)S(1)}, f32[12,24]{1,0:T(8,128)}, u32[]{:S(2)}) copy-start(f32[12,24]{1,0:T(8,128)} %param.22) | copy-start | bytes 3460
  579.1 54.1 %copy-start.26 = (f32[12,24]{1,0:T(8,128)S(1)}, f32[12,24]{1,0:T(8,128)}, u32[]{:S(2)}) copy-start(f32[12,24]{1,0:T(8,128)} %param.28) | copy-start | bytes 3460
  579.1 55.6 %copy-start.14 = (f32[120,768]{1,0:T(8,128)S(1)}, f32[120,768]{1,0:T(8,128)}, u32[]{:S(2)}) copy-start(f32[120,768]{1,0:T(8,128)} %param.21) | copy-start | bytes 1105924
  579.1 55.6 %copy-start.15 = (f32[120,768]{1,0:T(8,128)S(1)}, f32[120,768]{1,0:T(8,128)}, u32[]{:S(2)}) copy-start(f32[120,768]{1,0:T(8,128)} %reduce-scatter.6.cloned.1.call-done) | copy-start | bytes 1105924
  579.2 55.6 %copy-start.22 = (f32[120,768]{1,0:T(8,128)S(1)}, f32[120,768]{1,0:T(8,128)}, u32[]{:S(2)}) copy-start(f32[120,768]{1,0:T(8,128)} %param.27) | copy-start | bytes 1105924
  579.2 55.5 %copy-start.23 = (f32[120,768]{1,0:T(8,128)S(1)}, f32[120,768]{1,0:T(8,128)}, u32[]{:S(2)}) copy-start(f32[120,768]{1,0:T(8,128)} %param.24) | copy-start | bytes 1105924
  579.2 56.8 %copy-start.12 = (f32[24,5376]{1,0:T(8,128)S(1)}, f32[24,5376]{1,0:T(8,128)}, u32[]{:S(2)}) copy-start(f32[24,5376]{1,0:T(8,128)} %param.20) | copy-start | bytes 1548292
  579.2 56.8 %copy-start.13 = (f32[24,5376]{1,0:T(8,128)S(1)}, f32[24,5376]{1,0:T(8,128)}, u32[]{:S(2)}) copy-start(f32[24,5376]{1,0:T(8,128)} %reduce-scatter.4.cloned.1.call-done) | copy-start | bytes 1548292
  579.2 56.8 %copy-start.20 = (f32[24,5376]{1,0:T(8,128)S(1)}, f32[24,5376]{1,0:T(8,128)}, u32[]{:S(2)}) copy-start(f32[24,5376]{1,0:T(8,128)} %param.26) | copy-start | bytes 1548292
  579.2 56.8 %copy-start.21 = (f32[24,5376]{1,0:T(8,128)S(1)}, f32[24,5376]{1,0:T(8,128)}, u32[]{:S(2)}) copy-start(f32[24,5376]{1,0:T(8,128)} %param.23) | copy-start | bytes 1548292
Sparse Core Ops, SparseCore 0:
  11.6 80.3 all-gather.3
  95.5 66.3 all-gather.5
  231.2 146.7 reduce-scatter.5
  385.2 190.0 reduce-scatter.3
where the time goes:
time: 656 us; the launch traced here: 646 us
  waiting for transfers between devices  195 us (30%)
  matrix products  154 us (23%)
  blocking collectives  151 us (23%)
  local copies, waits for them, and re-layouts  75.2 us (11%)
  other arithmetic  51.4 us (8%)
  between operations  19.3 us (3%)
    reduce_scatter x1, waiting for transfers between devices, body(): lax.psum_scatter(full_in, ('dp', 'fsdp'), scatter_dimension=0, tiled=True)  181 us
    all_gather x1, blocking collectives, body(): lax.all_gather(low_small, ('dp', 'fsdp'), axis=1, tiled=True)  71.6 us
    unnamed x74, local copies, waits for them, and re-layouts  61.7 us
    unnamed x1, blocking collectives  39.7 us
    psum x1, blocking collectives, body(): total_squares = lax.psum(local_squares, ('dp', 'fsdp'))  39.3 us
    sub x1, matrix products, backward(): grad_probs - jnp.sum(attn_probs * grad_probs, axis=2, keepdims=True)  28.2 us
    dot_general x1, matrix products, forward(): jnp.dot(hidden_low, weight_in[:, 3 * model_width:], preferred_element_typ...  23.9 us
    broadcast_in_dim x1, other arithmetic, body(): scores.astype(jnp.bfloat16)[None]  17.7 us
  transfers between devices with their start and end apart: 4, of which 2 were waited for; matrix products, arithmetic and copies ran while one was open for 29% of the time, Pallas kernels for 0%

commit v1 on v0

--- a/solution.py
+++ b/solution.py
@@ -14,6 +14,20 @@
 rate_vector = 0.25
 decay_matrix = 0.01
 masked_fill = -1e30
+
+
+def order_lots_all(dimension_no, packet):
+    w_next, mixed_arr = (lax.axis_size(("dp", "fsdp")), lax.axis_index(("dp", "fsdp")))
+    value_now, odd = (packet, 1)
+    while odd < w_next:
+        known = lax.ppermute(
+            value_now, ("dp", "fsdp"), list(map(lambda it: (it, it ^ odd), range(w_next)))
+        )
+        v1 = jnp.concatenate([value_now, known], axis=dimension_no)
+        finding = jnp.concatenate([known, value_now], axis=dimension_no)
+        value_now = jnp.where(mixed_arr & odd == 0, v1, finding)
+        odd = 2 * odd
+    return value_now
 
 
 def gelu_exact(upward):
@@ -254,7 +268,7 @@
     low_small = vectors.astype(jnp.bfloat16)
     gathered = (
         lax.all_gather(low_in, ("dp", "fsdp"), axis=0, tiled=True),
-        lax.all_gather(low_out, ("dp", "fsdp"), axis=0, tiled=True),
+        order_lots_all(0, low_out),
         lax.all_gather(low_small, ("dp", "fsdp"), axis=1, tiled=True),
     )
     segments = segment_ids[0]

time: 656 us -> 751 us (1.14)
  waiting for transfers between devices: 195 us -> 243 us
  matrix products: 154 us -> 182 us
  other arithmetic: 51.4 us -> 63.2 us
  starting transfers between devices: 0.16 us -> 9.99 us
    ppermute x0 -> x5, waiting for transfers between devices: none -> 60.6 us  [order_lots_all(): lax.ppermute(value_now, ('dp', 'fsdp'), list(map(lambda it: (it, it ^ odd...]
    dot_general x1 -> x2, matrix products: 3.45 us -> 29.9 us  [forward(): jnp.dot(activated, weight_out[model_width:], preferred_element_type=jnp.f...]
    all_gather x1, waiting for transfers between devices: 14.3 us -> 0.01 us  [body(): lax.all_gather(low_out, ('dp', 'fsdp'), axis=0, tiled=True)]
    select_n x0 -> x5, other arithmetic: none -> 12 us  [order_lots_all(): value_now = jnp.where(mixed_arr & odd == 0, v1, finding)]
    ppermute x0 -> x5, starting transfers between devices: none -> 9.83 us  [order_lots_all(): lax.ppermute(value_now, ('dp', 'fsdp'), list(map(lambda it: (it, it ^ odd...]
    unnamed x74 -> x104, local copies, waits for them, and re-layouts: 61.7 us -> 63.2 us
  transfers between devices with their start and end apart: 4 -> 9, of which waited for: 2 -> 5; matrix products, arithmetic and copies ran while one was open for 29% -> 31% of each run, Pallas kernels for 0% -> 0%
where the time goes in v1:
time: 751 us; the launch traced here: 740 us
  waiting for transfers between devices  243 us (32%)
  matrix products  182 us (24%)
  blocking collectives  145 us (19%)
  local copies, waits for them, and re-layouts  77.3 us (10%)
  other arithmetic  63.2 us (8%)
  between operations  19.5 us (3%)
  starting transfers between devices  9.99 us (1%)
    reduce_scatter x1, waiting for transfers between devices, body(): lax.psum_scatter(full_in, ('dp', 'fsdp'), scatter_dimension=0, tiled=True)  182 us
    all_gather x1, blocking collectives, body(): lax.all_gather(low_small, ('dp', 'fsdp'), axis=1, tiled=True)  68.5 us
    unnamed x104, local copies, waits for them, and re-layouts  63.2 us
    ppermute x5, waiting for transfers between devices, order_lots_all(): lax.ppermute(value_now, ('dp', 'fsdp'), list(map(lambda it: (it, it ^ odd...  60.6 us
    psum x1, blocking collectives, body(): total_squares = lax.psum(local_squares, ('dp', 'fsdp'))  39.2 us
    unnamed x1, blocking collectives  37.8 us
    dot_general x2, matrix products, forward(): jnp.dot(activated, weight_out[model_width:], preferred_element_type=jnp.f...  29.9 us
    sub x1, matrix products, backward(): grad_probs - jnp.sum(attn_probs * grad_probs, axis=2, keepdims=True)  28.1 us
  transfers between devices with their start and end apart: 9, of which 5 were waited for; matrix products, arithmetic and copies ran while one was open for 31% of the time, Pallas kernels for 0%

profile of v1, /device:TPU:0, one launch (start us, length us, event | category | flops | bytes accessed | tf_op | source)
XLA Modules:
  0.0 740.4 jit_solution(7509389229638593081)
XLA Ops:
  7.3 1.8 convert_element_type.147
  10.1 3.0 collective-permute-start
  13.1 4.6 collective-permute-done
  17.8 1.9 collective-permute-start.1
  19.7 10.2 %collective-permute-done.1 = bf16[240,768]{1,0:T(8,128)(2,1)S(1)} collective-permute-done((bf16[240,768]{1,0:T(8,128)(2,1)S(1)}, bf16[240,768]{1,0:T(8,128)(2,1)S(1)}, u32[]{:S(2)}, u32[]{:S(2)}) %collective-permute-start.1) | collective-permute-done | bytes 368672 | tf_op jit(solution)/shard_map/ppermute | solution.py:23
  30.2 3.0 collective-permute-start.2
  33.3 43.3 %collective-permute-done.2 = bf16[480,768]{1,0:T(8,128)(2,1)S(1)} collective-permute-done((bf16[480,768]{1,0:T(8,128)(2,1)S(1)}, bf16[480,768]{1,0:T(8,128)(2,1)S(1)}, u32[]{:S(2)}, u32[]{:S(2)}) %collective-permute-start.2) | collective-permute-done | bytes 737312 | tf_op jit(solution)/shard_map/ppermute | solution.py:23
  78.4 2.4 collective-permute-done.3
  80.7 3.9 maximum_select_fusion.1
  84.7 1.8 collective-permute-start.4
  86.6 68.5 %all-gather = bf16[32,24,12]{1,2,0:T(8,128)(2,1)S(1)} all-gather(bf16[1,24,12]{1,2,0:T(8,128)(2,1)S(1)} %convert_bitcast_fusion.1), channel_id=1, replica_groups=mesh['dp'=4,'fsdp'=8] {'dp','fsdp'}, dimensions={0}, use_global_device_ids=true | all-gather | bytes 19008 | tf_op jit(solution)/shard_map/all_gather | solution.py:272
  155.5 13.8 %copy.85 = bf16[1,12,640,640]{2,3,1,0:T(8,128)(2,1)} copy(bf16[1,12,640,640]{3,2,1,0:T(8,128)(2,1)} %param.16) | data formatting | bytes 19660800 | tf_op args[1]
  170.2 7.1 maximum_select_fusion
  177.4 4.8 fusion.78
  184.9 1.9 copy.82
  186.8 12.2 %select_reduce_fusion = (f32[12,640]{1,0:T(8,128)S(1)}, f32[12,640,640]{1,2,0:T(8,128)}) fusion(pred[640,640]{0,1:T(8,128)(4,1)S(1)} %broadcast_compare_fusion, bf16[1,12,640,640]{2,3,1,0:T(8,128)(2,1)} %copy.85, bf16[640,12,64]{0,2,1:T(8,128)(2,1)S(1)} %bitcast.64, bf16[640,12,64]{0,2,1:T(8,128)(2,1)S(1)} %bitcast.62), kind=kOutput, calls=%fused_computation.11 | convolution fusion | flops 653713920 | bytes 31897600 | tf_op jit(solution)/shard_map/qhd,khd->hqk/dot_general | solution.py:68
  199.0 17.6 %convert_bitcast_fusion = (bf16[1,12,640,640]{2,3,1,0:T(8,128)(2,1)}, f32[12,640]{1,0:T(8,128)S(1)}) fusion(f32[12,640,640]{1,2,0:T(8,128)} %get-tuple-element.143, f32[12,640]{1,0:T(8,128)S(1)} %get-tuple-element.142, pred[640,640]{0,1:T(8,128)(4,1)S(1)} %broadcast_compare_fusion), kind=kLoop, calls=%fused_computation.19 | loop fusion | flops 19653120 | bytes 29962240 | tf_op jit(solution)/shard_map/broadcast_in_dim | solution.py:313
  216.6 9.7 %fusion.106 = bf16[12,64,640]{2,1,0:T(8,128)(2,1)S(1)} fusion(bf16[640,12,64]{0,2,1:T(8,128)(2,1)S(1)} %bitcast.68, f32[12,640,640]{1,2,0:T(8,128)} %get-tuple-element.143, f32[12,640]{1,0:T(8,128)S(1)} %get-tuple-element.138, f32[12,640]{1,0:T(8,128)S(1)} %get-tuple-element.142, pred[640,640]{0,1:T(8,128)(4,1)S(1)} %broadcast_compare_fusion), kind=kOutput, calls=%fused_computation.153 | convolution fusion | flops 649297920 | bytes 22097920 | tf_op jit(solution)/shard_map/hqk,khd->qhd/dot_general | solution.py:80
  226.3 2.7 fusion.178
  230.4 26.5 %fusion.179 = (f32[640]{0:T(1024)S(1)}, f32[640,768]{1,0:T(8,128)S(1)}) fusion(f32[768]{0:T(1024)S(1)} %get-tuple-element.110, bf16[3840,768]{1,0:T(8,128)(2,1)} %maximum_select_fusion, f32[3072]{0:T(1024)S(1)} %add.249, bf16[768,5376]{1,0:T(8,128)(2,1)} %all-gather.4.cloned.1.call-done, f32[640,768]{1,0:T(8,128)} %copy-done.19, ...), kind=kOutput, calls=%fused_computation.254 | convolution fusion | flops 6175456768 | bytes 15387136 | tf_op jit(solution)/shard_map/dot_general | solution.py:98
  258.1 3.0 fusion.176
  261.5 23.7 %multiply_convert_fusion = (bf16[640,3072]{1,0:T(8,128)(2,1)S(1)}, f32[640,3072]{1,0:T(8,128)}, f32[640,3072]{1,0:T(8,128)}) fusion(f32[3072]{0:T(1024)S(1)} %add.249, bf16[768,5376]{1,0:T(8,128)(2,1)} %all-gather.4.cloned.1.call-done, f32[640,768]{1,0:T(8,128)S(1)} %get-tuple-element.145, f32[640]{0:T(1024)S(1)} %add_rsqrt_fusion.1, ...), kind=kOutput, calls=%fused_computation.31 | convolution fusion | flops 3152117760 | bytes 26369024 | tf_op jit(solution)/shard_map/dot_general | solution.py:93
  285.2 3.4 fusion.177
  290.1 2.4 convert_reduce_fusion.2
  292.5 6.8 fusion.130
  299.2 10.4 %convert_reduce_fusion = (f32[3072]{0:T(1024)S(1)}, bf16[640,3072]{1,0:T(8,128)(2,1)S(1)}) fusion(f32[640,3072]{1,0:T(8,128)} %get-tuple-element.136, bf16[3840,768]{1,0:T(8,128)(2,1)} %all-gather.6.cloned.1.call-done, f32[640,768]{1,0:T(8,128)S(1)} %get-tuple-element.132, f32[640,3072]{1,0:T(8,128)} %get-tuple-element.146, f32[3072]{0:T(1024)S(1)} %add.249), kind=kOutput, calls=%fused_computation.29 | convolution fusion | flops 3053810688 | bytes 26370048 | tf_op jit(solution)/shard_map/td,fd->tf/dot_general | solution.py:147
  309.7 3.8 multiply_reduce_fusion.1
  315.5 2.5 fusion.127
  318.0 9.5 %pad_maximum_fusion.1 = f32[3840,768]{1,0:T(8,128)} fusion(f32[3072,768]{1,0:T(8,128)} %fusion.130, f32[768,768]{1,0:T(8,128)} %fusion.127), kind=kLoop, calls=%fused_computation.13 | loop fusion | flops 2949120 | bytes 23592960 | tf_op jit(solution)/shard_map/concatenate | solution.py:230
  327.5 14.6 %copy.88 = bf16[1,12,640,640]{2,3,1,0:T(8,128)(2,1)} copy(bf16[1,12,640,640]{3,2,1,0:T(8,128)(2,1)} %param.19) | data formatting | bytes 19660800 | tf_op args[4]
  342.1 3.0 convolution_convert_fusion
  346.5 28.1 %fusion.1 = bf16[12,640,640]{1,2,0:T(8,128)(2,1)} fusion(f32[12,640,640]{1,2,0:T(8,128)} %get-tuple-element.143, bf16[1,12,640,640]{2,3,1,0:T(8,128)(2,1)} %copy.88, f32[12,640]{1,0:T(8,128)S(1)} %log_add_fusion, pred[640,640]{0,1:T(8,128)(4,1)S(1)} %copy-done.14, bf16[640,12,64]{0,2,1:T(8,128)(2,1)} %bitcast.75, bf16[640,12,64]{0,2,1:T(8,128)(2,1)} %bitcast.69), kind=kOutput, calls=%fused_computation.2 | convolution fusion | flops 1307451520 | bytes 41728000 | tf_op jit(solution)/shard_map/sub | solution.py:178
  374.7 6.4 convert_reduce_fusion.5
  382.5 3.2 multiply_convert_fusion.1
  385.7 11.5 %convert_reduce_fusion.4 = (f32[12,64]{1,0:T(8,128)S(1)}, bf16[12,64,640]{2,1,0:T(8,128)(2,1)S(1)}) fusion(bf16[640,12,64]{0,2,1:T(8,128)(2,1)S(1)} %bitcast.76, f32[12,640,640]{1,2,0:T(8,128)} %get-tuple-element.143, f32[12,640]{1,0:T(8,128)S(1)} %log_add_fusion, pred[640,640]{0,1:T(8,128)(4,1)S(1)} %copy-done.14), kind=kOutput, calls=%fused_computation.129 | convolution fusion | flops 645364992 | bytes 22070272 | tf_op jit(solution)/shard_map/hqk,qhd->khd/dot_general | solution.py:198
  398.2 7.9 %convolution_bitcast_fusion = f32[768,2304]{0,1:T(8,128)} fusion(bf16[640,768]{1,0:T(8,128)(2,1)S(1)} %copy-done.44, bf16[640,768]{0,1:T(8,128)(2,1)S(1)} %bitcast.83, bf16[640,768]{0,1:T(8,128)(2,1)S(1)} %bitcast.73, bf16[640,768]{0,1:T(8,128)(2,1)S(1)} %bitcast.66), kind=kOutput, calls=%fused_computation.61 | convolution fusion | flops 2273771520 | bytes 11010048 | tf_op jit(solution)/shard_map/td,tc->dc/dot_general | solution.py:208
  406.2 8.2 %copy.92 = f32[768,2304]{1,0:T(8,128)} copy(f32[768,2304]{0,1:T(8,128)} %convolution_bitcast_fusion) | data formatting | bytes 14155776 | tf_op jit(solution)/shard_map/td,tc->dc/dot_general | solution.py:208
  414.4 6.5 fusion.165
  420.9 6.0 pad_maximum_fusion
  427.8 14.3 %copy.94 = bf16[1,12,640,640]{3,2,1,0:T(8,128)(2,1)} copy(bf16[1,12,640,640]{2,3,1,0:T(8,128)(2,1)} %bitcast.61) | data formatting | bytes 19660800
  442.2 37.8 %all-reduce = f32[12,768]{1,0:T(8,128)S(1)} all-reduce(f32[12,768]{1,0:T(8,128)S(1)} %concatenate.55), channel_id=4, replica_groups=mesh['dp'=4,'fsdp'=8] {'dp','fsdp'}, use_global_device_ids=true, to_apply=%region_28.29.clone | all-reduce | flops 9216 | bytes 73728
  480.7 6.0 add_convert_fusion.1
  486.8 1.7 multiply_reduce_fusion.9
  488.5 181.9 %reduce-scatter.4.cloned.1.call-done = f32[24,5376]{1,0:T(8,128)} async-done(((f32[768,5376]{1,0:T(8,128)}), f32[24,5376]{1,0:T(8,128)}) %reduce-scatter.4.cloned.1.call-update) | async-done | bytes 516112 | tf_op jit(solution)/shard_map/reduce_scatter | solution.py:288
  670.4 1.8 multiply_reduce_fusion.8
  674.2 13.9 %copy.93 = bf16[1,12,640,640]{3,2,1,0:T(8,128)(2,1)} copy(bf16[1,12,640,640]{2,3,1,0:T(8,128)(2,1)} %get-tuple-element.137) | data formatting | bytes 19660800
  688.2 39.2 %psum.7 = f32[]{:T(128)} all-reduce(f32[]{:T(128)S(6)} %add.273), channel_id=1, replica_groups=mesh['dp'=4,'fsdp'=8] {'dp','fsdp'}, use_global_device_ids=true, to_apply=%region_30.31 | all-reduce | flops 1 | bytes 8 | tf_op jit(solution)/shard_map/psum | solution.py:297
  730.9 1.5 fusion.172
  (164 shorter events, 21.0 us)
Async XLA Ops:
  7.2 79.4 %copy-start.38 = (f32[12,24]{1,0:T(8,128)S(1)}, f32[12,24]{1,0:T(8,128)}, u32[]{:S(2)}) copy-start(f32[12,24]{1,0:T(8,128)} %param.22) | copy-start | bytes 3460
  7.2 148.3 %copy-start.42 = (s32[1,640]{1,0:T(1,128)S(1)}, s32[1,640]{1,0:T(1,128)}, u32[]{:S(2)}) copy-start(s32[1,640]{1,0:T(1,128)} %param.17) | copy-start | bytes 7684
  7.2 170.1 %all-gather.4.cloned.1.call-start = ((), (), s32[]{:S(2)}) async-start(), calls=%async_computation.2 | async-start | bytes 8515584 | tf_op jit(solution)/shard_map/all_gather | solution.py:270
  9.0 249.1 %all-gather.6.cloned.1.call-start = ((), (), s32[]{:S(2)}) async-start(), calls=%async_computation.3 | async-start | bytes 6082560 | tf_op jit(solution)/shard_map/all_gather | solution.py:280
  10.1 76.4 %copy-start.20 = (bf16[120,768]{1,0:T(8,128)(2,1)}, bf16[120,768]{1,0:T(8,128)(2,1)S(1)}, u32[]{:S(2)}) copy-start(bf16[120,768]{1,0:T(8,128)(2,1)S(1)} %convert_element_type.158) | copy-start | bytes 552964
  10.1 7.6 %collective-permute-start = (bf16[120,768]{1,0:T(8,128)(2,1)S(1)}, bf16[120,768]{1,0:T(8,128)(2,1)S(1)}, u32[]{:S(2)}, u32[]{:S(2)}) collective-permute-start(bf16[120,768]{1,0:T(8,128)(2,1)S(1)} %convert_element_type.158), channel_id=1, source_target_pairs={{0,1},{1,0},{2,3},{3,2},{4,5},{5,4},{6,7},{7,6},{8,9},{9,8},{10,11... | collective-permute-start | bytes 552968 | tf_op jit(solution)/shard_map/ppermute | solution.py:23
  17.8 12.1 %collective-permute-start.1 = (bf16[240,768]{1,0:T(8,128)(2,1)S(1)}, bf16[240,768]{1,0:T(8,128)(2,1)S(1)}, u32[]{:S(2)}, u32[]{:S(2)}) collective-permute-start(bf16[240,768]{1,0:T(8,128)(2,1)S(1)} %maximum_select_fusion.4), channel_id=1, source_target_pairs={{0,2},{1,3},{2,0},{3,1},{4,6},{5,7},{6,4},{7,5},{8,10},{9,11},{10,... | collective-permute-start | bytes 1105928 | tf_op jit(solution)/shard_map/ppermute | solution.py:23
  30.2 46.4 %collective-permute-start.2 = (bf16[480,768]{1,0:T(8,128)(2,1)S(1)}, bf16[480,768]{1,0:T(8,128)(2,1)S(1)}, u32[]{:S(2)}, u32[]{:S(2)}) collective-permute-start(bf16[480,768]{1,0:T(8,128)(2,1)S(1)} %maximum_select_fusion.3), channel_id=1, source_target_pairs={{0,4},{1,5},{2,6},{3,7},{4,0},{5,1},{6,2},{7,3},{8,12},{9,13},{10,... | collective-permute-start | bytes 2211848 | tf_op jit(solution)/shard_map/ppermute | solution.py:23
  77.3 3.5 collective-permute-start.3
  84.7 85.6 %collective-permute-start.4 = (bf16[1920,768]{1,0:T(8,128)(2,1)S(1)}, bf16[1920,768]{1,0:T(8,128)(2,1)}, u32[]{:S(2)}, u32[]{:S(2)}) collective-permute-start(bf16[1920,768]{1,0:T(8,128)(2,1)S(1)} %maximum_select_fusion.1), channel_id=1, source_target_pairs={{0,16},{1,17},{2,18},{3,19},{4,20},{5,21},{6,22},{7,23},{8,24},{9,... | collective-permute-start | bytes 8847368 | tf_op jit(solution)/shard_map/ppermute | solution.py:23
  86.5 400.2 %reduce-scatter.6.cloned.1.call-start = ((), (), s32[]{:S(2)}) async-start(), calls=%async_computation.5 | async-start | bytes 12165120 | tf_op jit(solution)/shard_map/reduce_scatter | solution.py:289
  170.2 46.4 %copy-start.13 = (pred[640,640]{0,1:T(8,128)(4,1)}, pred[640,640]{0,1:T(8,128)(4,1)S(1)}, u32[]{:S(2)}) copy-start(pred[640,640]{0,1:T(8,128)(4,1)S(1)} %broadcast_compare_fusion) | copy-start | bytes 1228804
  184.2 14.8 %copy-start.4 = (bf16[640,768]{0,1:T(8,128)(2,1)}, bf16[640,768]{0,1:T(8,128)(2,1)S(1)}, u32[]{:S(2)}) copy-start(bf16[640,768]{0,1:T(8,128)(2,1)S(1)} %copy.83) | copy-start | bytes 2949124
  184.9 14.1 %copy-start.2 = (bf16[640,768]{0,1:T(8,128)(2,1)}, bf16[640,768]{0,1:T(8,128)(2,1)S(1)}, u32[]{:S(2)}) copy-start(bf16[640,768]{0,1:T(8,128)(2,1)S(1)} %copy.84) | copy-start | bytes 2949124
  186.8 29.8 %copy-start.23 = (bf16[640,768]{0,1:T(8,128)(2,1)}, bf16[640,768]{0,1:T(8,128)(2,1)S(1)}, u32[]{:S(2)}) copy-start(bf16[640,768]{0,1:T(8,128)(2,1)S(1)} %copy.82) | copy-start | bytes 2949124
  199.0 17.6 %copy-start.30 = (f32[12,640]{1,0:T(8,128)}, f32[12,640]{1,0:T(8,128)S(1)}, u32[]{:S(2)}) copy-start(f32[12,640]{1,0:T(8,128)S(1)} %get-tuple-element.142) | copy-start | bytes 92164
  216.6 9.7 %copy-start.34 = (f32[12,640]{1,0:T(8,128)}, f32[12,640]{1,0:T(8,128)S(1)}, u32[]{:S(2)}) copy-start(f32[12,640]{1,0:T(8,128)S(1)} %get-tuple-element.138) | copy-start | bytes 92164
  216.6 9.7 %copy-start.43 = (bf16[640,768]{1,0:T(8,128)(2,1)S(1)}, bf16[640,768]{1,0:T(8,128)(2,1)}, u32[]{:S(2)}) copy-start(bf16[640,768]{1,0:T(8,128)(2,1)} %param.15) | copy-start | bytes 2949124
  230.4 27.8 %copy-start.25 = (bf16[12,64,640]{2,1,0:T(8,128)(2,1)S(1)}, bf16[12,64,640]{2,1,0:T(8,128)(2,1)}, u32[]{:S(2)}) copy-start(bf16[12,64,640]{2,1,0:T(8,128)(2,1)} %copy-done.24) | copy-start | bytes 2949124
  258.1 27.1 %slice-start.2 = ((s8[5898240]{0:T(1024)(128)(4,1)}), s8[4194304]{0:T(1024)(128)(4,1)S(1)}, s32[]{:S(2)}) async-start(s8[5898240]{0:T(1024)(128)(4,1)} %bitcast.81), calls=%async_computation.8 | async-start | bytes 8388608
  261.5 23.7 %slice-start.3 = ((s8[5898240]{0:T(1024)(128)(4,1)}), s8[1703936]{0:T(1024)(128)(4,1)S(1)}, s32[]{:S(2)}) async-start(s8[5898240]{0:T(1024)(128)(4,1)} %bitcast.81), calls=%async_computation.9 | async-start | bytes 3407872
  285.2 4.9 copy-start.7
  292.5 17.2 %slice-start = ((s8[8257536]{0:T(1024)(128)(4,1)}), s8[4194304]{0:T(1024)(128)(4,1)S(1)}, s32[]{:S(2)}) async-start(s8[8257536]{0:T(1024)(128)(4,1)} %bitcast.79), calls=%async_computation.6 | async-start | bytes 8388608
  299.2 10.5 %slice-start.1 = ((s8[8257536]{0:T(1024)(128)(4,1)}), s8[4063232]{0:T(1024)(128)(4,1)S(1)}, s32[]{:S(2)}) async-start(s8[8257536]{0:T(1024)(128)(4,1)} %bitcast.79), calls=%async_computation.7 | async-start | bytes 8126464
  327.5 19.0 %copy-start.31 = (f32[12,640]{1,0:T(8,128)S(1)}, f32[12,640]{1,0:T(8,128)}, u32[]{:S(2)}) copy-start(f32[12,640]{1,0:T(8,128)} %copy-done.30) | copy-start | bytes 92164
  327.5 19.0 %copy-start.35 = (f32[12,640]{1,0:T(8,128)S(1)}, f32[12,640]{1,0:T(8,128)}, u32[]{:S(2)}) copy-start(f32[12,640]{1,0:T(8,128)} %copy-done.34) | copy-start | bytes 92164
  327.5 19.0 %copy-start.14 = (pred[640,640]{0,1:T(8,128)(4,1)S(1)}, pred[640,640]{0,1:T(8,128)(4,1)}, u32[]{:S(2)}) copy-start(pred[640,640]{0,1:T(8,128)(4,1)} %copy-done.13) | copy-start | bytes 1228804
  327.5 342.9 %reduce-scatter.4.cloned.1.call-start = ((), (), s32[]{:S(2)}) async-start(), calls=%async_computation.4 | async-start | bytes 17031168 | tf_op jit(solution)/shard_map/reduce_scatter | solution.py:288
  346.5 28.1 %copy-start.3 = (bf16[640,768]{0,1:T(8,128)(2,1)S(1)}, bf16[640,768]{0,1:T(8,128)(2,1)}, u32[]{:S(2)}) copy-start(bf16[640,768]{0,1:T(8,128)(2,1)} %copy-done.2) | copy-start | bytes 2949124
  374.7 7.6 %copy-start = (bf16[12,640,640]{1,2,0:T(8,128)(2,1)S(1)}, bf16[12,640,640]{1,2,0:T(8,128)(2,1)}, u32[]{:S(2)}) copy-start(bf16[12,640,640]{1,2,0:T(8,128)(2,1)} %fusion.1) | copy-start | bytes 29491204
  374.7 7.8 %copy-start.5 = (bf16[640,768]{0,1:T(8,128)(2,1)S(1)}, bf16[640,768]{0,1:T(8,128)(2,1)}, u32[]{:S(2)}) copy-start(bf16[640,768]{0,1:T(8,128)(2,1)} %copy-done.4) | copy-start | bytes 2949124
  382.5 14.8 %copy-start.15 = (bf16[12,64,640]{2,1,0:T(8,128)(2,1)}, bf16[12,64,640]{2,1,0:T(8,128)(2,1)S(1)}, u32[]{:S(2)}) copy-start(bf16[12,64,640]{2,1,0:T(8,128)(2,1)S(1)} %get-tuple-element.155) | copy-start | bytes 2949124
  385.7 11.6 %copy-start.26 = (bf16[12,64,640]{2,1,0:T(8,128)(2,1)}, bf16[12,64,640]{2,1,0:T(8,128)(2,1)S(1)}, u32[]{:S(2)}) copy-start(bf16[12,64,640]{2,1,0:T(8,128)(2,1)S(1)} %multiply_convert_fusion.1) | copy-start | bytes 2949124
  385.7 12.5 %copy-start.44 = (bf16[640,768]{1,0:T(8,128)(2,1)S(1)}, bf16[640,768]{1,0:T(8,128)(2,1)}, u32[]{:S(2)}) copy-start(bf16[640,768]{1,0:T(8,128)(2,1)} %param.15) | copy-start | bytes 2949124
  414.4 6.5 copy-start.1
  427.8 52.9 %copy-start.9 = (f32[640,768]{1,0:T(8,128)S(1)}, f32[640,768]{1,0:T(8,128)}, u32[]{:S(2)}) copy-start(f32[640,768]{1,0:T(8,128)} %copy-done.8) | copy-start | bytes 5898244
  427.8 52.9 %copy-start.16 = (bf16[12,64,640]{2,1,0:T(8,128)(2,1)S(1)}, bf16[12,64,640]{2,1,0:T(8,128)(2,1)}, u32[]{:S(2)}) copy-start(bf16[12,64,640]{2,1,0:T(8,128)(2,1)} %copy-done.15) | copy-start | bytes 2949124
  480.0 6.7 copy-start.36
  674.1 54.0 %copy-start.39 = (f32[12,24]{1,0:T(8,128)S(1)}, f32[12,24]{1,0:T(8,128)}, u32[]{:S(2)}) copy-start(f32[12,24]{1,0:T(8,128)} %param.22) | copy-start | bytes 3460
  674.1 54.0 %copy-start.41 = (f32[12,24]{1,0:T(8,128)S(1)}, f32[12,24]{1,0:T(8,128)}, u32[]{:S(2)}) copy-start(f32[12,24]{1,0:T(8,128)} %param.28) | copy-start | bytes 3460
  674.1 55.4 %copy-start.21 = (f32[120,768]{1,0:T(8,128)S(1)}, f32[120,768]{1,0:T(8,128)}, u32[]{:S(2)}) copy-start(f32[120,768]{1,0:T(8,128)} %param.21) | copy-start | bytes 1105924
  674.1 55.4 %copy-start.22 = (f32[120,768]{1,0:T(8,128)S(1)}, f32[120,768]{1,0:T(8,128)}, u32[]{:S(2)}) copy-start(f32[120,768]{1,0:T(8,128)} %reduce-scatter.6.cloned.1.call-done) | copy-start | bytes 1105924
  674.2 55.4 %copy-start.32 = (f32[120,768]{1,0:T(8,128)S(1)}, f32[120,768]{1,0:T(8,128)}, u32[]{:S(2)}) copy-start(f32[120,768]{1,0:T(8,128)} %param.27) | copy-start | bytes 1105924
  674.2 55.4 %copy-start.33 = (f32[120,768]{1,0:T(8,128)S(1)}, f32[120,768]{1,0:T(8,128)}, u32[]{:S(2)}) copy-start(f32[120,768]{1,0:T(8,128)} %param.24) | copy-start | bytes 1105924
  674.2 56.7 %copy-start.17 = (f32[24,5376]{1,0:T(8,128)S(1)}, f32[24,5376]{1,0:T(8,128)}, u32[]{:S(2)}) copy-start(f32[24,5376]{1,0:T(8,128)} %param.20) | copy-start | bytes 1548292
  674.2 56.6 %copy-start.18 = (f32[24,5376]{1,0:T(8,128)S(1)}, f32[24,5376]{1,0:T(8,128)}, u32[]{:S(2)}) copy-start(f32[24,5376]{1,0:T(8,128)} %reduce-scatter.4.cloned.1.call-done) | copy-start | bytes 1548292
  674.2 56.6 %copy-start.28 = (f32[24,5376]{1,0:T(8,128)S(1)}, f32[24,5376]{1,0:T(8,128)}, u32[]{:S(2)}) copy-start(f32[24,5376]{1,0:T(8,128)} %param.26) | copy-start | bytes 1548292
  674.2 56.6 %copy-start.29 = (f32[24,5376]{1,0:T(8,128)S(1)}, f32[24,5376]{1,0:T(8,128)}, u32[]{:S(2)}) copy-start(f32[24,5376]{1,0:T(8,128)} %param.23) | copy-start | bytes 1548292
  (11 other events, 28.8 us)
Sparse Core Ops, SparseCore 0:
  11.6 112.4 all-gather.3
  127.7 68.6 all-gather.5
  327.6 145.2 reduce-scatter.5
  480.2 190.0 reduce-scatter.3
